TPU v7x, 128 devices: a whole 4x4x4 slice. The times are simulated.
128 devices in a mesh: pts: 16 (over z_hi, x, core), mem: 8 (over z_lo, y).
Axes of the slice: x: 4, y: 4, z: 4 (z_hi: 2, z_lo: 2; z = z_hi * 2 + z_lo), core: 2. Of those that a mesh axis runs over, the one named last changes fastest.
Arguments:
- ensemble: bfloat16 [128, 128, 8192], P('mem', None, 'pts'), may hold values from -4 to 4
- increment: float32 [128, 8192], P(None, 'pts'), may hold values from -8 to 8
- obs_weight: float32 [128, 8192], P(None, 'pts'), may hold values from 0.3 to 3
- vertical: bfloat16 [128, 128], replicated, may hold values from -0.5 to 0.5
- block_table: bfloat16 [12, 128, 128], replicated, may hold values from -0.15625 to 0.15625
- block_cols: int32 [64, 12], replicated, may hold values from 0 to 63, as said below
Outputs:
- weighted: float32 [128, 8192], P(None, 'pts')
- applied: float32 [128, 8192], P(None, 'pts')
Inputs may be any that keep to these rules, and one draw needn't show every extreme that they name: `block_cols`: row r begins with r itself, and its 12 entries are different block indices.
All inputs are finite; a program needn't handle non-finite values.
Results may differ from a plain program's by a relative error of at most 0.012.
Values may be sent and summed in bfloat16 or wider, within the bound.
A program may use at most 128 MiB of HBM per device.

v0:
```python
import jax
import jax.numpy as jnp
from jax import lax
from jax.sharding import PartitionSpec as P


def sent_to_all(shard, axis):
    copies = jnp.broadcast_to(shard, (lax.axis_size(axis), *shard.shape))
    return lax.all_to_all(copies, axis, split_axis=0, concat_axis=0, tiled=True)


def taken_together(shard, axis):
    everything = sent_to_all(shard, axis)
    return jnp.sum(everything, axis=0)


def localize(values, block_table, block_cols):
    leading = values.shape[:-1]
    npoints = values.shape[-1]
    blk_width = block_table.shape[-1]
    flattened = values.reshape(-1, npoints // blk_width, blk_width)

    def add_slot(column, running):
        chosen = lax.dynamic_index_in_dim(block_cols, column, 1, keepdims=False)
        picked = jnp.take(flattened, chosen, axis=1)
        kernel = lax.dynamic_index_in_dim(block_table, column, 0, keepdims=False)
        return running + jnp.einsum(
            "rnk,lk->rnl", picked, kernel, preferred_element_type=jnp.float32
        )

    running = lax.fori_loop(
        0, block_table.shape[0], add_slot, jnp.zeros(flattened.shape, jnp.float32)
    )
    return running.reshape(leading + (npoints,)).astype(jnp.bfloat16)


def per_device(ensemble, increment, obs_weight, vertical, block_table, block_cols):
    spread_levels = lax.all_to_all(ensemble, "pts", split_axis=1, concat_axis=2, tiled=True)

    def horiz_items(moved):
        return localize(moved, block_table, block_cols)

    def cov_local(field_now):
        product = (ensemble.astype(jnp.float32) * field_now).astype(jnp.bfloat16)
        vert_mixed = jnp.einsum(
            "lk,mkp->mlp", vertical, product, preferred_element_type=jnp.float32
        ).astype(jnp.bfloat16)
        level_local = horiz_items(
            lax.all_to_all(vert_mixed, "pts", split_axis=1, concat_axis=2, tiled=True)
        )
        level_sums = jnp.sum(
            spread_levels.astype(jnp.float32) * level_local.astype(jnp.float32), axis=0
        )
        return lax.all_to_all(level_sums, "pts", split_axis=1, concat_axis=0, tiled=True)

    def member_total(member_terms, use_weights):
        summed = taken_together(member_terms, "mem")
        if use_weights:
            summed = summed * obs_weight
        return summed

    weighted = member_total(cov_local(increment), True)
    applied = member_total(cov_local(weighted), False)
    return (weighted, applied)


def solution(mesh):
    return jax.shard_map(
        per_device,
        mesh=mesh,
        in_specs=(P("mem", None, "pts"), P(None, "pts"), P(None, "pts"), P(), P(), P()),
        out_specs=(P(None, "pts"), P(None, "pts")),
        check_vma=False,
    )
```

profile of v0, /device:TPU:6, one launch (start us, length us, event | category | flops | bytes accessed | tf_op | source)
XLA Modules:
  0.0 429.0 jit_solution(13721641971145328131)
XLA Ops:
  6.7 8.2 %all-to-all-start.1 = ((bf16[16,128,512]{2,0,1:T(8,128)(2,1)}), bf16[16,128,512]{2,0,1:T(8,128)(2,1)}, u32[]{:S(2)}, u32[]{:S(2)}) async-start(bf16[16,128,512]{2,0,1:T(8,128)(2,1)} %copy.51), calls=%async_computation.1 | async-start | bytes 4194304 | tf_op jit(solution)/shard_map/all_to_all | solution.py:49
  17.5 23.6 %all-to-all-done.1 = bf16[16,128,512]{2,0,1:T(8,128)(2,1)} async-done(((bf16[16,128,512]{2,0,1:T(8,128)(2,1)}), bf16[16,128,512]{2,0,1:T(8,128)(2,1)}, u32[]{:S(2)}, u32[]{:S(2)}) %all-to-all-start.1) | async-done | bytes 2097184 | tf_op jit(solution)/shard_map/all_to_all | solution.py:49
  41.1 7.8 %all-to-all-start = ((bf16[16,128,512]{2,0,1:T(8,128)(2,1)}), bf16[16,128,512]{2,0,1:T(8,128)(2,1)}, u32[]{:S(2)}, u32[]{:S(2)}) async-start(bf16[16,128,512]{2,0,1:T(8,128)(2,1)} %copy.48), calls=%async_computation | async-start | bytes 4194304 | tf_op jit(solution)/shard_map/all_to_all | solution.py:38
  58.5 96.6 %while.28 = (s32[]{:T(128)}, f32[128,64,128]{2,0,1:T(8,128)}, s32[64,12]{0,1:T(8,128)}, bf16[128,64,128]{2,0,1:T(8,128)(2,1)}, bf16[12,128,128]{2,1,0:T(8,128)(2,1)}, /*index=5*/s32[]{:T(128)}, s32[]{:T(128)}) while((s32[]{:T(128)}, f32[128,64,128]{2,0,1:T(8,128)}, s32[64,12]{0,1:T(8,128)}, bf16[128,64,128]{2,0,1:T(8,128)(2,1)}, ...), condition=%wide.region_1.0_spmd.clone, body=%wide.region_0.2_spmd.clone.sunk | while | flops 271582592 | bytes 14718683 | solution.py:31
  68.5 4.9 %select_add_fusion.4 = f32[128,64,128]{2,0,1:T(8,128)} fusion(f32[128,64,128]{2,0,1:T(8,128)} %get-tuple-element.361, bf16[64,128,128]{2,1,0:T(8,128)(2,1)S(1)} %gather_fusion, pred[64]{0:T(512)(128)(4,1)S(1)} %get-tuple-element.345, pred[]{:T(512)S(6)} %compare.6, bf16[12,128,128]{2,1,0:T(8,128)(2,1)} %get-tuple-element.371, s32[]{:T(128)} %get-tuple-element.360), kind=kOutput, calls=%fused_computation.2.clone.1 | convolution fusion | flops 271581184 | bytes 10519105 | tf_op jit(solution)/shard_map/while/body/eval_jaxpr/rnk,lk->rnl/dot_general | solution.py:27
  76.6 4.9 %select_add_fusion.4 = f32[128,64,128]{2,0,1:T(8,128)} fusion(f32[128,64,128]{2,0,1:T(8,128)} %get-tuple-element.361, bf16[64,128,128]{2,1,0:T(8,128)(2,1)S(1)} %gather_fusion, pred[64]{0:T(512)(128)(4,1)S(1)} %get-tuple-element.345, pred[]{:T(512)S(6)} %compare.6, bf16[12,128,128]{2,1,0:T(8,128)(2,1)} %get-tuple-element.371, s32[]{:T(128)} %get-tuple-element.360), kind=kOutput, calls=%fused_computation.2.clone.1 | convolution fusion | flops 271581184 | bytes 10519105 | tf_op jit(solution)/shard_map/while/body/eval_jaxpr/rnk,lk->rnl/dot_general | solution.py:27
  93.0 4.9 %select_add_fusion.4 = f32[128,64,128]{2,0,1:T(8,128)} fusion(f32[128,64,128]{2,0,1:T(8,128)} %get-tuple-element.361, bf16[64,128,128]{2,1,0:T(8,128)(2,1)S(1)} %gather_fusion, pred[64]{0:T(512)(128)(4,1)S(1)} %get-tuple-element.345, pred[]{:T(512)S(6)} %compare.6, bf16[12,128,128]{2,1,0:T(8,128)(2,1)} %get-tuple-element.371, s32[]{:T(128)} %get-tuple-element.360), kind=kOutput, calls=%fused_computation.2.clone.1 | convolution fusion | flops 271581184 | bytes 10519105 | tf_op jit(solution)/shard_map/while/body/eval_jaxpr/rnk,lk->rnl/dot_general | solution.py:27
  101.1 4.9 %select_add_fusion.4 = f32[128,64,128]{2,0,1:T(8,128)} fusion(f32[128,64,128]{2,0,1:T(8,128)} %get-tuple-element.361, bf16[64,128,128]{2,1,0:T(8,128)(2,1)S(1)} %gather_fusion, pred[64]{0:T(512)(128)(4,1)S(1)} %get-tuple-element.345, pred[]{:T(512)S(6)} %compare.6, bf16[12,128,128]{2,1,0:T(8,128)(2,1)} %get-tuple-element.371, s32[]{:T(128)} %get-tuple-element.360), kind=kOutput, calls=%fused_computation.2.clone.1 | convolution fusion | flops 271581184 | bytes 10519105 | tf_op jit(solution)/shard_map/while/body/eval_jaxpr/rnk,lk->rnl/dot_general | solution.py:27
  109.3 4.9 %select_add_fusion.4 = f32[128,64,128]{2,0,1:T(8,128)} fusion(f32[128,64,128]{2,0,1:T(8,128)} %get-tuple-element.361, bf16[64,128,128]{2,1,0:T(8,128)(2,1)S(1)} %gather_fusion, pred[64]{0:T(512)(128)(4,1)S(1)} %get-tuple-element.345, pred[]{:T(512)S(6)} %compare.6, bf16[12,128,128]{2,1,0:T(8,128)(2,1)} %get-tuple-element.371, s32[]{:T(128)} %get-tuple-element.360), kind=kOutput, calls=%fused_computation.2.clone.1 | convolution fusion | flops 271581184 | bytes 10519105 | tf_op jit(solution)/shard_map/while/body/eval_jaxpr/rnk,lk->rnl/dot_general | solution.py:27
  117.5 4.9 %select_add_fusion.4 = f32[128,64,128]{2,0,1:T(8,128)} fusion(f32[128,64,128]{2,0,1:T(8,128)} %get-tuple-element.361, bf16[64,128,128]{2,1,0:T(8,128)(2,1)S(1)} %gather_fusion, pred[64]{0:T(512)(128)(4,1)S(1)} %get-tuple-element.345, pred[]{:T(512)S(6)} %compare.6, bf16[12,128,128]{2,1,0:T(8,128)(2,1)} %get-tuple-element.371, s32[]{:T(128)} %get-tuple-element.360), kind=kOutput, calls=%fused_computation.2.clone.1 | convolution fusion | flops 271581184 | bytes 10519105 | tf_op jit(solution)/shard_map/while/body/eval_jaxpr/rnk,lk->rnl/dot_general | solution.py:27
  125.7 4.9 %select_add_fusion.4 = f32[128,64,128]{2,0,1:T(8,128)} fusion(f32[128,64,128]{2,0,1:T(8,128)} %get-tuple-element.361, bf16[64,128,128]{2,1,0:T(8,128)(2,1)S(1)} %gather_fusion, pred[64]{0:T(512)(128)(4,1)S(1)} %get-tuple-element.345, pred[]{:T(512)S(6)} %compare.6, bf16[12,128,128]{2,1,0:T(8,128)(2,1)} %get-tuple-element.371, s32[]{:T(128)} %get-tuple-element.360), kind=kOutput, calls=%fused_computation.2.clone.1 | convolution fusion | flops 271581184 | bytes 10519105 | tf_op jit(solution)/shard_map/while/body/eval_jaxpr/rnk,lk->rnl/dot_general | solution.py:27
  133.8 4.9 %select_add_fusion.4 = f32[128,64,128]{2,0,1:T(8,128)} fusion(f32[128,64,128]{2,0,1:T(8,128)} %get-tuple-element.361, bf16[64,128,128]{2,1,0:T(8,128)(2,1)S(1)} %gather_fusion, pred[64]{0:T(512)(128)(4,1)S(1)} %get-tuple-element.345, pred[]{:T(512)S(6)} %compare.6, bf16[12,128,128]{2,1,0:T(8,128)(2,1)} %get-tuple-element.371, s32[]{:T(128)} %get-tuple-element.360), kind=kOutput, calls=%fused_computation.2.clone.1 | convolution fusion | flops 271581184 | bytes 10519105 | tf_op jit(solution)/shard_map/while/body/eval_jaxpr/rnk,lk->rnl/dot_general | solution.py:27
  142.0 4.9 %select_add_fusion.4 = f32[128,64,128]{2,0,1:T(8,128)} fusion(f32[128,64,128]{2,0,1:T(8,128)} %get-tuple-element.361, bf16[64,128,128]{2,1,0:T(8,128)(2,1)S(1)} %gather_fusion, pred[64]{0:T(512)(128)(4,1)S(1)} %get-tuple-element.345, pred[]{:T(512)S(6)} %compare.6, bf16[12,128,128]{2,1,0:T(8,128)(2,1)} %get-tuple-element.371, s32[]{:T(128)} %get-tuple-element.360), kind=kOutput, calls=%fused_computation.2.clone.1 | convolution fusion | flops 271581184 | bytes 10519105 | tf_op jit(solution)/shard_map/while/body/eval_jaxpr/rnk,lk->rnl/dot_general | solution.py:27
  150.2 4.9 %select_add_fusion.4 = f32[128,64,128]{2,0,1:T(8,128)} fusion(f32[128,64,128]{2,0,1:T(8,128)} %get-tuple-element.361, bf16[64,128,128]{2,1,0:T(8,128)(2,1)S(1)} %gather_fusion, pred[64]{0:T(512)(128)(4,1)S(1)} %get-tuple-element.345, pred[]{:T(512)S(6)} %compare.6, bf16[12,128,128]{2,1,0:T(8,128)(2,1)} %get-tuple-element.371, s32[]{:T(128)} %get-tuple-element.360), kind=kOutput, calls=%fused_computation.2.clone.1 | convolution fusion | flops 271581184 | bytes 10519105 | tf_op jit(solution)/shard_map/while/body/eval_jaxpr/rnk,lk->rnl/dot_general | solution.py:27
  161.9 4.9 %reshape.43 = f32[16,8,16,512]{3,2,1,0:T(8,128)} reshape(f32[128,64,128]{2,1,0:T(8,128)} %copy.55) | data formatting | bytes 8388608 | tf_op jit(solution)/shard_map/convert_element_type | solution.py:52
  166.8 6.2 %fusion.20 = f32[8,16,512]{2,0,1:T(8,128)S(1)} fusion(f32[16,8,16,512]{3,2,1,0:T(8,128)} %reshape.43, bf16[16,128,512]{2,0,1:T(8,128)(2,1)} %all-to-all-done), kind=kLoop, calls=%fused_computation.33 | loop fusion | flops 3080192 | bytes 6553600 | tf_op jit(solution)/shard_map/reduce_sum | solution.py:51
  173.0 14.0 %all_to_all.81 = f32[8,16,512]{2,0,1:T(8,128)S(1)} all-to-all(f32[8,16,512]{2,0,1:T(8,128)S(1)} %fusion.20), channel_id=1, replica_groups=mesh['pts'=16,'mem'=8] {'pts'}, dimensions={1} | all-to-all | bytes 524288 | tf_op jit(solution)/shard_map/all_to_all | solution.py:54
  187.3 32.4 %all_to_all.82 = f32[8,128,512]{2,1,0:T(8,128)} all-to-all(f32[8,128,512]{2,1,0:T(8,128)S(1)} %broadcast_in_dim.17), channel_id=1, replica_groups=mesh['pts'=16,'mem'=8] {'mem'}, dimensions={0} | all-to-all | bytes 4194304 | tf_op jit(solution)/shard_map/all_to_all | solution.py:9
  228.7 5.3 %all-to-all-start.4 = ((bf16[16,128,512]{2,0,1:T(8,128)(2,1)}), bf16[16,128,512]{2,0,1:T(8,128)(2,1)S(1)}, u32[]{:S(2)}, u32[]{:S(2)}) async-start(bf16[16,128,512]{2,0,1:T(8,128)(2,1)} %copy.58), calls=%async_computation.4 | async-start | bytes 4194304 | tf_op jit(solution)/shard_map/all_to_all | solution.py:49
  234.1 26.0 %all-to-all-done.4 = bf16[16,128,512]{2,0,1:T(8,128)(2,1)S(1)} async-done(((bf16[16,128,512]{2,0,1:T(8,128)(2,1)}), bf16[16,128,512]{2,0,1:T(8,128)(2,1)S(1)}, u32[]{:S(2)}, u32[]{:S(2)}) %all-to-all-start.4) | async-done | bytes 2097184 | tf_op jit(solution)/shard_map/all_to_all | solution.py:49
  268.3 96.6 %while.29 = (s32[]{:T(128)}, f32[128,64,128]{2,0,1:T(8,128)}, s32[64,12]{0,1:T(8,128)}, bf16[128,64,128]{2,0,1:T(8,128)(2,1)}, bf16[12,128,128]{2,1,0:T(8,128)(2,1)}, /*index=5*/s32[]{:T(128)}, s32[]{:T(128)}) while((s32[]{:T(128)}, f32[128,64,128]{2,0,1:T(8,128)}, s32[64,12]{0,1:T(8,128)}, bf16[128,64,128]{2,0,1:T(8,128)(2,1)}, ...), condition=%wide.region_5.7_spmd.clone, body=%wide.region_4.6_spmd.clone.sunk | while | flops 271582592 | bytes 14718683 | solution.py:31
  278.3 4.9 %select_add_fusion.5 = f32[128,64,128]{2,0,1:T(8,128)} fusion(f32[128,64,128]{2,0,1:T(8,128)} %get-tuple-element.382, bf16[64,128,128]{2,1,0:T(8,128)(2,1)S(1)} %gather_fusion.1, pred[64]{0:T(512)(128)(4,1)S(1)} %get-tuple-element.352, pred[]{:T(512)S(6)} %compare.7, bf16[12,128,128]{2,1,0:T(8,128)(2,1)} %get-tuple-element.392, s32[]{:T(128)} %get-tuple-element.381), kind=kOutput, calls=%fused_computation.14.clone.1 | convolution fusion | flops 271581184 | bytes 10519105 | tf_op jit(solution)/shard_map/while/body/eval_jaxpr/rnk,lk->rnl/dot_general | solution.py:27
  294.6 4.9 %select_add_fusion.5 = f32[128,64,128]{2,0,1:T(8,128)} fusion(f32[128,64,128]{2,0,1:T(8,128)} %get-tuple-element.382, bf16[64,128,128]{2,1,0:T(8,128)(2,1)S(1)} %gather_fusion.1, pred[64]{0:T(512)(128)(4,1)S(1)} %get-tuple-element.352, pred[]{:T(512)S(6)} %compare.7, bf16[12,128,128]{2,1,0:T(8,128)(2,1)} %get-tuple-element.392, s32[]{:T(128)} %get-tuple-element.381), kind=kOutput, calls=%fused_computation.14.clone.1 | convolution fusion | flops 271581184 | bytes 10519105 | tf_op jit(solution)/shard_map/while/body/eval_jaxpr/rnk,lk->rnl/dot_general | solution.py:27
  302.8 4.9 %select_add_fusion.5 = f32[128,64,128]{2,0,1:T(8,128)} fusion(f32[128,64,128]{2,0,1:T(8,128)} %get-tuple-element.382, bf16[64,128,128]{2,1,0:T(8,128)(2,1)S(1)} %gather_fusion.1, pred[64]{0:T(512)(128)(4,1)S(1)} %get-tuple-element.352, pred[]{:T(512)S(6)} %compare.7, bf16[12,128,128]{2,1,0:T(8,128)(2,1)} %get-tuple-element.392, s32[]{:T(128)} %get-tuple-element.381), kind=kOutput, calls=%fused_computation.14.clone.1 | convolution fusion | flops 271581184 | bytes 10519105 | tf_op jit(solution)/shard_map/while/body/eval_jaxpr/rnk,lk->rnl/dot_general | solution.py:27
  319.1 4.9 %select_add_fusion.5 = f32[128,64,128]{2,0,1:T(8,128)} fusion(f32[128,64,128]{2,0,1:T(8,128)} %get-tuple-element.382, bf16[64,128,128]{2,1,0:T(8,128)(2,1)S(1)} %gather_fusion.1, pred[64]{0:T(512)(128)(4,1)S(1)} %get-tuple-element.352, pred[]{:T(512)S(6)} %compare.7, bf16[12,128,128]{2,1,0:T(8,128)(2,1)} %get-tuple-element.392, s32[]{:T(128)} %get-tuple-element.381), kind=kOutput, calls=%fused_computation.14.clone.1 | convolution fusion | flops 271581184 | bytes 10519105 | tf_op jit(solution)/shard_map/while/body/eval_jaxpr/rnk,lk->rnl/dot_general | solution.py:27
  327.3 4.9 %select_add_fusion.5 = f32[128,64,128]{2,0,1:T(8,128)} fusion(f32[128,64,128]{2,0,1:T(8,128)} %get-tuple-element.382, bf16[64,128,128]{2,1,0:T(8,128)(2,1)S(1)} %gather_fusion.1, pred[64]{0:T(512)(128)(4,1)S(1)} %get-tuple-element.352, pred[]{:T(512)S(6)} %compare.7, bf16[12,128,128]{2,1,0:T(8,128)(2,1)} %get-tuple-element.392, s32[]{:T(128)} %get-tuple-element.381), kind=kOutput, calls=%fused_computation.14.clone.1 | convolution fusion | flops 271581184 | bytes 10519105 | tf_op jit(solution)/shard_map/while/body/eval_jaxpr/rnk,lk->rnl/dot_general | solution.py:27
  343.6 4.9 %select_add_fusion.5 = f32[128,64,128]{2,0,1:T(8,128)} fusion(f32[128,64,128]{2,0,1:T(8,128)} %get-tuple-element.382, bf16[64,128,128]{2,1,0:T(8,128)(2,1)S(1)} %gather_fusion.1, pred[64]{0:T(512)(128)(4,1)S(1)} %get-tuple-element.352, pred[]{:T(512)S(6)} %compare.7, bf16[12,128,128]{2,1,0:T(8,128)(2,1)} %get-tuple-element.392, s32[]{:T(128)} %get-tuple-element.381), kind=kOutput, calls=%fused_computation.14.clone.1 | convolution fusion | flops 271581184 | bytes 10519105 | tf_op jit(solution)/shard_map/while/body/eval_jaxpr/rnk,lk->rnl/dot_general | solution.py:27
  351.8 4.9 %select_add_fusion.5 = f32[128,64,128]{2,0,1:T(8,128)} fusion(f32[128,64,128]{2,0,1:T(8,128)} %get-tuple-element.382, bf16[64,128,128]{2,1,0:T(8,128)(2,1)S(1)} %gather_fusion.1, pred[64]{0:T(512)(128)(4,1)S(1)} %get-tuple-element.352, pred[]{:T(512)S(6)} %compare.7, bf16[12,128,128]{2,1,0:T(8,128)(2,1)} %get-tuple-element.392, s32[]{:T(128)} %get-tuple-element.381), kind=kOutput, calls=%fused_computation.14.clone.1 | convolution fusion | flops 271581184 | bytes 10519105 | tf_op jit(solution)/shard_map/while/body/eval_jaxpr/rnk,lk->rnl/dot_general | solution.py:27
  371.7 4.9 %reshape.44 = f32[16,8,16,512]{3,2,1,0:T(8,128)} reshape(f32[128,64,128]{2,1,0:T(8,128)} %copy.62) | data formatting | bytes 8388608 | tf_op jit(solution)/shard_map/convert_element_type | solution.py:52
  376.7 6.2 %fusion.21 = f32[8,16,512]{2,0,1:T(8,128)S(1)} fusion(f32[16,8,16,512]{3,2,1,0:T(8,128)} %reshape.44, bf16[16,128,512]{2,0,1:T(8,128)(2,1)} %all-to-all-done), kind=kLoop, calls=%fused_computation.34 | loop fusion | flops 3080192 | bytes 6553600 | tf_op jit(solution)/shard_map/reduce_sum | solution.py:51
  382.8 14.6 %all_to_all.83 = f32[8,16,512]{2,0,1:T(8,128)S(1)} all-to-all(f32[8,16,512]{2,0,1:T(8,128)S(1)} %fusion.21), channel_id=1, replica_groups=mesh['pts'=16,'mem'=8] {'pts'}, dimensions={1} | all-to-all | bytes 524288 | tf_op jit(solution)/shard_map/all_to_all | solution.py:54
  397.7 30.4 %all_to_all.84 = f32[8,128,512]{2,1,0:T(8,128)S(1)} all-to-all(f32[8,128,512]{2,1,0:T(8,128)S(1)} %broadcast_in_dim.18), channel_id=1, replica_groups=mesh['pts'=16,'mem'=8] {'mem'}, dimensions={0} | all-to-all | bytes 4194304 | tf_op jit(solution)/shard_map/all_to_all | solution.py:9
  (114 shorter events, 159.9 us)
Async XLA Ops:
  0.6 0.8 copy-start
  6.7 8.2 %copy-start.2 = (bf16[16,128,512]{2,1,0:T(8,128)(2,1)S(1)}, bf16[16,128,512]{2,1,0:T(8,128)(2,1)}, u32[]{:S(2)}) copy-start(bf16[16,128,512]{2,1,0:T(8,128)(2,1)} %param.12) | copy-start | bytes 6291460
  6.7 34.3 %all-to-all-start.1 = ((bf16[16,128,512]{2,0,1:T(8,128)(2,1)}), bf16[16,128,512]{2,0,1:T(8,128)(2,1)}, u32[]{:S(2)}, u32[]{:S(2)}) async-start(bf16[16,128,512]{2,0,1:T(8,128)(2,1)} %copy.51), calls=%async_computation.1 | async-start | bytes 4194304 | tf_op jit(solution)/shard_map/all_to_all | solution.py:49
  41.1 125.8 %all-to-all-start = ((bf16[16,128,512]{2,0,1:T(8,128)(2,1)}), bf16[16,128,512]{2,0,1:T(8,128)(2,1)}, u32[]{:S(2)}, u32[]{:S(2)}) async-start(bf16[16,128,512]{2,0,1:T(8,128)(2,1)} %copy.48), calls=%async_computation | async-start | bytes 4194304 | tf_op jit(solution)/shard_map/all_to_all | solution.py:38
  219.7 2.0 copy-start.5
  219.7 2.3 copy-start.3
  222.0 2.1 copy-start.4
  228.7 31.3 %all-to-all-start.4 = ((bf16[16,128,512]{2,0,1:T(8,128)(2,1)}), bf16[16,128,512]{2,0,1:T(8,128)(2,1)S(1)}, u32[]{:S(2)}, u32[]{:S(2)}) async-start(bf16[16,128,512]{2,0,1:T(8,128)(2,1)} %copy.58), calls=%async_computation.4 | async-start | bytes 4194304 | tf_op jit(solution)/shard_map/all_to_all | solution.py:49
  397.7 31.3 %copy-start.1 = (bf16[128,128]{1,0:T(8,128)(2,1)S(1)}, bf16[128,128]{1,0:T(8,128)(2,1)}, u32[]{:S(2)}) copy-start(bf16[128,128]{1,0:T(8,128)(2,1)} %param.15) | copy-start | bytes 98308
where the time goes:
time: 434 us; the launch traced here: 429 us
  matrix products  119 us (27%)
  local copies, waits for them, and re-layouts  109 us (25%)
  blocking collectives  91.5 us (21%)
  waiting for transfers between devices  49.6 us (11%)
  other arithmetic  37 us (9%)
  starting transfers between devices  21.3 us (5%)
    dot_general x24, matrix products, add_slot(): jnp.einsum('rnk,lk->rnl', picked, kernel, preferred_element_type=jnp.floa...  115 us
    all_to_all x2, blocking collectives, sent_to_all(): return lax.all_to_all(copies, axis, split_axis=0, concat_axis=0, tiled=True)  62.8 us
    gather x24, local copies, waits for them, and re-layouts, add_slot(): picked = jnp.take(flattened, chosen, axis=1)  61 us
    all_to_all x2, waiting for transfers between devices, cov_local(): lax.all_to_all(vert_mixed, 'pts', split_axis=1, concat_axis=2, tiled=True)  49.6 us
    all_to_all x2, blocking collectives, cov_local(): lax.all_to_all(level_sums, 'pts', split_axis=1, concat_axis=0, tiled=True)  28.6 us
    convert_element_type x4, local copies, waits for them, and re-layouts, cov_local(): level_local.astype(jnp.float32)  18.6 us
    and x24, other arithmetic, add_slot(): picked = jnp.take(flattened, chosen, axis=1)  16.7 us
    all_to_all x2, starting transfers between devices, cov_local(): lax.all_to_all(vert_mixed, 'pts', split_axis=1, concat_axis=2, tiled=True)  13.5 us
  transfers between devices with their start and end apart: 3, of which 2 were waited for; matrix products, arithmetic and copies ran while one was open for 28% of the time, Pallas kernels for 0%

commit v1 on v0

v1 whole, which is shorter than its diff:
```python
import jax
import jax.numpy as jnp
from jax import lax
from jax.experimental import pallas as pl
from jax.experimental.pallas import tpu as pltpu
from jax.sharding import PartitionSpec as P

MESH = pl.DeviceIdType.MESH
BF = jnp.bfloat16
F32 = jnp.float32

SPREAD = (
    (1, 1, 0), (0, 3, 0), (1, 3, 1), (0, 1, 1), (1, 0, 0), (0, 2, 0), (1, 2, 1), (0, 2, 1),
    (1, 2, 0), (1, 0, 1), (1, 3, 0), (0, 1, 0), (1, 1, 1), (0, 3, 1), (0, 0, 1),
)
PLANE = tuple((db, dz) for db in range(4) for dz in range(4) if (db, dz) != (0, 0))


def device(zhi, x, core, zlo, y):
    return ((zhi * 4 + x) * 2 + core, zlo * 4 + y)


def kernel(
    ens_hbm, inc_hbm, obs_hbm, vert_ref, table_ref, cols_ref,
    weighted_ref, applied_ref,
    ens, vl, tt, piece, obs,
    f1, f2, xo1, xo2, xi1, xi2, r1, r2, q1, q2, s1, s2, w1, w2, last,
    local_sem, es_sem, er_sem,
    gs1, gr1, gs2, gr2, gs3, gr3,
    cs, cr, as_, ar, bs, br, ls, lr,
):
    p, g = lax.axis_index("pts"), lax.axis_index("mem")
    zhi, x, core = p // 8, (p // 2) % 4, p % 2
    zlo, y = g // 4, g % 4
    zz = zhi * 2 + zlo
    partner = device(zhi, x, 1 - core, zlo, y)

    def pick(flat):
        return flat * y + (1 - flat) * x, flat * x + (1 - flat) * y

    def ring_peer(flat, a):
        return device(zhi, flat * x + (1 - flat) * a, core, zlo, flat * a + (1 - flat) * y)

    def plane_peer(flat, b, z):
        return device(z // 2, flat * b + (1 - flat) * x, core, z % 2, flat * y + (1 - flat) * b)

    def remote(src, dst, send, recv, to):
        return pltpu.make_async_remote_copy(
            src_ref=src, dst_ref=dst, send_sem=send, recv_sem=recv,
            device_id=to, device_id_type=MESH,
        )

    inc_copy = pltpu.make_async_copy(
        inc_hbm.at[pl.ds(pl.multiple_of(g * 16, 16), 16)], piece, local_sem.at[0])
    obs_copy = pltpu.make_async_copy(
        obs_hbm.at[pl.ds(pl.multiple_of(g * 16, 16), 16)], obs, local_sem.at[1])
    own_copy = pltpu.make_async_copy(ens_hbm.at[p], ens.at[p], local_sem.at[2])
    inc_copy.start()
    obs_copy.start()
    own_copy.start()

    spread_to = [
        device((zhi + dz) % 2, (x + dx) % 4, (core + dc) % 2, zlo, y) for dz, dx, dc in SPREAD
    ]
    by_core = 1 - core

    barrier = pltpu.get_barrier_semaphore()
    greet = list(spread_to)
    for flat in (1, by_core):
        a, b = pick(flat)
        greet += [ring_peer(flat, (a + d) % 4) for d in (1, 2, 3)]
        greet += [plane_peer(flat, (b + db) % 4, (zz + dz) % 4) for db, dz in PLANE]
    mem_peers = [(p, (g + d) % 8) for d in range(1, 8)]
    greet += mem_peers
    for to in greet:
        pl.semaphore_signal(barrier, inc=1, device_id=to, device_id_type=MESH)
    pl.semaphore_wait(barrier, len(greet))

    inc_copy.wait()

    def gather(n, f, flat, between):
        a, b = pick(flat)
        first = []
        for k, (db, dz) in enumerate(PLANE):
            mine = f.at[core, a, b, zz]
            copy = remote(mine, mine, gs1.at[n, k], gr1.at[n, b * 4 + zz],
                          plane_peer(flat, (b + db) % 4, (zz + dz) % 4))
            copy.start()
            first.append(copy)
        between()
        for db, dz in PLANE:
            bb, z2 = (b + db) % 4, (zz + dz) % 4
            slot = f.at[core, a, bb, z2]
            remote(slot, slot, gs1.at[n, 0], gr1.at[n, bb * 4 + z2], partner).wait_recv()
        second = []
        for d in (1, 2, 3):
            mine = f.at[core, a]
            copy = remote(mine, mine, gs2.at[n, d], gr2.at[n, a], ring_peer(flat, (a + d) % 4))
            copy.start()
            second.append(copy)
        third = []
        for d in range(4):
            aa = (a + d) % 4
            slot = f.at[core, aa]
            if d:
                remote(slot, slot, gs2.at[n, 0], gr2.at[n, aa], partner).wait_recv()
            copy = remote(slot, slot, gs3.at[n, d], gr3.at[n, aa], partner)
            copy.start()
            third.append(copy)
        return first + second + third

    def gather_rest(n, f):
        for a in range(4):
            slot = f.at[1 - core, a]
            remote(slot, slot, gs3.at[n, 0], gr3.at[n, a], partner).wait_recv()

    def field_at(f, flat, zhi2, x2, core2):
        rows = []
        for zl in range(2):
            for yy in range(4):
                rows.append(f[core2, flat * yy + (1 - flat) * x2, flat * x2 + (1 - flat) * yy, zhi2 * 2 + zl])
        return jnp.concatenate(rows, axis=0)

    def vertical_part(f, flat_of, core2, wait):
        flat = flat_of(core2)

        def one(i, carry):
            p2 = i * 2 + core2
            if wait:
                @pl.when(p2 != p)
                def _():
                    slot = ens.at[p2]
                    remote(slot, slot, es_sem.at[0], er_sem.at[p2], partner).wait_recv()
            field = field_at(f, flat, i // 4, i % 4, core2)
            product = (ens[p2].astype(F32) * field.astype(F32)).astype(BF)
            mixed = jnp.dot(vert_ref[...], product, preferred_element_type=F32).astype(BF)
            for k in range(4):
                vl[p2 * 4 + k] = mixed[:, k * 128:(k + 1) * 128]
            return carry

        lax.fori_loop(0, 8, one, 0)

    def horizontal(p2):
        parts = []
        for k in range(4):
            total = None
            for s in range(0, 12, 2):
                left = vl[cols_ref[(p2 * 4 + k) * 12 + s]]
                right = vl[cols_ref[(p2 * 4 + k) * 12 + s + 1]]
                term = jnp.dot(jnp.concatenate([left, right], axis=1),
                               tt[s * 128:(s + 2) * 128], preferred_element_type=F32)
                total = term if total is None else total + term
            parts.append(total.astype(BF))
        local = jnp.concatenate(parts, axis=1)
        return ens[p2].astype(F32) * local.astype(F32)

    def scatter(n, xo, xi, r, q, s_buf, w):
        flat = by_core
        a, b = pick(flat)

        def away(i, carry):
            x2, zh = i // 2, i % 2
            p2 = (zh * 4 + x2) * 2 + 1 - core
            xo[i] = horizontal(p2).astype(BF)
            remote(xo.at[i], xi.at[i], cs.at[n, i], cr.at[n, i], partner).start()
            return carry

        lax.fori_loop(0, 8, away, 0)

        def ring_copy(x2, yy):
            a2, b2 = flat * yy + (1 - flat) * x2, flat * x2 + (1 - flat) * yy
            return a2, remote(r.at[a2, b2], q.at[a, b2], as_.at[n, a2 * 4 + b2],
                              ar.at[n, a * 4 + b2], ring_peer(flat, a2))

        def keep(x2, carry):
            for zh in range(2):
                i = x2 * 2 + zh
                p2 = (zh * 4 + x2) * 2 + core
                mine = horizontal(p2)
                remote(xo.at[i], xi.at[i], cs.at[n, i], cr.at[n, i], partner).wait_recv()
                both = (mine + xi[i].astype(F32)).astype(BF)
                for zl in range(2):
                    for yy in range(4):
                        a2, b2 = flat * yy + (1 - flat) * x2, flat * x2 + (1 - flat) * yy
                        r[a2, b2, zh * 2 + zl] = both[zl * 64 + yy * 16:zl * 64 + yy * 16 + 16]
            for yy in range(4):
                a2, copy = ring_copy(x2, yy)

                @pl.when(a2 != a)
                def _():
                    copy.start()
            return carry

        lax.fori_loop(0, 4, keep, 0)

        def plane_copy(b2, z2):
            return remote(s_buf.at[b2, z2], w.at[b * 4 + zz], bs.at[n, b2 * 4 + z2],
                          br.at[n, b * 4 + zz], plane_peer(flat, b2, z2))

        for b2 in range(4):
            for d in (1, 2, 3):
                aa = (a + d) % 4
                slot = q.at[aa, b2]
                remote(slot, slot, as_.at[n, 0], ar.at[n, aa * 4 + b2], partner).wait_recv()
            total = r[a, b2].astype(F32)
            for d in (1, 2, 3):
                total = total + q[(a + d) % 4, b2].astype(F32)
            s_buf[b2] = total.astype(BF)
            for z2 in range(4):
                @pl.when(jnp.logical_or(b != b2, zz != z2))
                def _():
                    plane_copy(b2, z2).start()
        total = s_buf[b, zz].astype(F32)
        for db, dz in PLANE:
            k = (b + db) % 4 * 4 + (zz + dz) % 4
            remote(w.at[k], w.at[k], bs.at[n, 0], br.at[n, k], partner).wait_recv()
            total = total + w[k].astype(F32)

        def finish():
            for i in range(8):
                remote(xo.at[i], xi.at[i], cs.at[n, i], cr.at[n, i], partner).wait_send()
            for x2 in range(4):
                for yy in range(4):
                    a2, copy = ring_copy(x2, yy)

                    @pl.when(a2 != a)
                    def _():
                        copy.wait_send()
            for b2 in range(4):
                for z2 in range(4):
                    @pl.when(jnp.logical_or(b != b2, zz != z2))
                    def _():
                        plane_copy(b2, z2).wait_send()

        return total, finish

    a1, b1 = pick(1)
    f1[core, a1, b1, zz] = piece[...].astype(BF)
    spread = []

    def start_spread():
        for k, (dz, dx, dc) in enumerate(SPREAD):
            to = spread_to[k]
            copy = remote(ens_hbm.at[to[0]], ens.at[p], es_sem.at[k], er_sem.at[p], to)
            copy.start()
            spread.append(copy)
        for s in range(12):
            tt[s * 128:(s + 1) * 128] = table_ref[s].T

    sent = gather(0, f1, 1, start_spread)
    own_copy.wait()
    vertical_part(f1, lambda c: 1, core, True)
    gather_rest(0, f1)
    vertical_part(f1, lambda c: 1, 1 - core, True)
    first, finish1 = scatter(0, xo1, xi1, r1, q1, s1, w1)

    obs_copy.wait()
    a2, b2 = pick(by_core)
    f2[core, a2, b2, zz] = (first * obs[...]).astype(BF)
    sent += gather(1, f2, by_core, lambda: None)
    vertical_part(f2, lambda c: 1 - c, core, False)
    weighted_ref[...] = field_at(f2, by_core, zhi, x, core).astype(F32)
    gather_rest(1, f2)
    vertical_part(f2, lambda c: 1 - c, 1 - core, False)
    second, finish2 = scatter(1, xo2, xi2, r2, q2, s2, w2)

    last[g] = second
    out = []
    for k, to in enumerate(mem_peers):
        copy = remote(last.at[g], last.at[g], ls.at[k], lr.at[g], to)
        copy.start()
        out.append(copy)
    finish1()
    finish2()
    for copy in spread + sent:
        copy.wait_send()
    for d in range(1, 8):
        k = (g + d) % 8
        remote(last.at[k], last.at[k], ls.at[0], lr.at[k], partner).wait_recv()
    for k in range(8):
        applied_ref[k * 16:(k + 1) * 16] = last[k]
    for copy in out:
        copy.wait_send()


def per_device(ensemble, increment, obs_weight, vertical, block_table, block_cols):
    dma = pltpu.SemaphoreType.DMA
    vmem = pl.BlockSpec(memory_space=pltpu.VMEM)
    hbm = pl.BlockSpec(memory_space=pl.ANY)
    field = pltpu.VMEM((2, 4, 4, 4, 16, 512), BF)
    return pl.pallas_call(
        kernel,
        out_shape=(jax.ShapeDtypeStruct((128, 512), F32), jax.ShapeDtypeStruct((128, 512), F32)),
        in_specs=[hbm, hbm, hbm, vmem, vmem, pl.BlockSpec(memory_space=pltpu.SMEM)],
        out_specs=(vmem, vmem),
        scratch_shapes=[
            pltpu.VMEM((16, 128, 512), BF),
            pltpu.VMEM((64, 128, 128), BF),
            pltpu.VMEM((12 * 128, 128), BF),
            pltpu.VMEM((16, 512), F32),
            pltpu.VMEM((16, 512), F32),
            field, field,
        ] + [pltpu.VMEM((8, 128, 512), BF)] * 4
        + [pltpu.VMEM((4, 4, 4, 16, 512), BF)] * 4
        + [pltpu.VMEM((4, 4, 16, 512), BF)] * 2
        + [pltpu.VMEM((16, 16, 512), BF)] * 2
        + [
            pltpu.VMEM((8, 16, 512), F32),
            dma((3,)), dma((15,)), dma((16,)),
            dma((2, 15)), dma((2, 16)), dma((2, 4)), dma((2, 4)), dma((2, 4)), dma((2, 4)),
            dma((2, 8)), dma((2, 8)), dma((2, 16)), dma((2, 16)), dma((2, 16)), dma((2, 16)),
            dma((7,)), dma((8,)),
        ],
        compiler_params=pltpu.CompilerParams(
            collective_id=0, has_side_effects=True, vmem_limit_bytes=48 * 1024 * 1024),
        name="covariance",
    )(ensemble, increment, obs_weight, vertical, block_table, block_cols.reshape(-1))


def solution(mesh):
    return jax.shard_map(
        per_device,
        mesh=mesh,
        in_specs=(P("mem", None, "pts"), P(None, "pts"), P(None, "pts"), P(), P(), P()),
        out_specs=(P(None, "pts"), P(None, "pts")),
        check_vma=False,
    )
```

time: 434 us -> 114 us (0.26); the launches traced: 429 us -> 114 us
  matrix products: 119 us -> 0 us
  Pallas kernels: 0 us -> 106 us
  local copies, waits for them, and re-layouts: 109 us -> 7.53 us
  blocking collectives: 91.5 us -> 0 us
  waiting for transfers between devices: 49.6 us -> 0 us
  other arithmetic: 37 us -> 0 us
  starting transfers between devices: 21.3 us -> 0 us
    dot_general x26 -> x0, matrix products: 119 us -> none  [the longest x24 115 us: add_slot(): jnp.einsum('rnk,lk->rnl', picked, kernel, preferred_element_type=jnp.floa...]
    pallas_call x0 -> x1, Pallas kernels: none -> 106 us  [per_device(): pl.pallas_call(kernel, out_shape=(jax.ShapeDtypeStruct((128, 512), F32),...]
    all_to_all x4 -> x0, blocking collectives: 91.5 us -> none  [the longest x2 62.8 us: sent_to_all(): return lax.all_to_all(copies, axis, split_axis=0, concat_axis=0, tiled=True)]
    gather x24 -> x0, local copies, waits for them, and re-layouts: 61 us -> none  [add_slot(): picked = jnp.take(flattened, chosen, axis=1)]
    all_to_all x3 -> x0, waiting for transfers between devices: 49.6 us -> none  [the longest x2 49.6 us: cov_local(): lax.all_to_all(vert_mixed, 'pts', split_axis=1, concat_axis=2, tiled=True)]
    convert_element_type x6 -> x0, local copies, waits for them, and re-layouts: 26.2 us -> none  [the longest x4 18.6 us: cov_local(): level_local.astype(jnp.float32)]
    all_to_all x3 -> x0, starting transfers between devices: 21.3 us -> none  [the longest x2 13.5 us: cov_local(): lax.all_to_all(vert_mixed, 'pts', split_axis=1, concat_axis=2, tiled=True)]
    and x24 -> x0, other arithmetic: 16.7 us -> none  [add_slot(): picked = jnp.take(flattened, chosen, axis=1)]
  transfers between devices with their start and end apart: 3 -> 0, of which waited for: 2 -> 0; matrix products, arithmetic and copies ran while one was open for 28% -> 0% of each run, Pallas kernels for 0% -> 0%
where the time goes in v1:
time: 114 us
  Pallas kernels  106 us (93%)
  local copies, waits for them, and re-layouts  7.53 us (7%)
    pallas_call x1, Pallas kernels, per_device(): pl.pallas_call(kernel, out_shape=(jax.ShapeDtypeStruct((128, 512), F32),...  106 us
    unnamed x13, local copies, waits for them, and re-layouts  7.43 us

profile of v1, /device:TPU:6, one launch (start us, length us, event | category | flops | bytes accessed | tf_op | source)
XLA Modules:
  0.0 113.7 jit_solution(590844570243365143)
XLA Ops:
  0.6 0.8 copy.8
  1.4 0.1 reshape.7.cols_ref
  1.5 0.0 copy-start
  1.5 1.6 %copy-done = bf16[16,128,512]{2,1,0:T(8,128)(2,1)S(1)} copy-done((bf16[16,128,512]{2,1,0:T(8,128)(2,1)S(1)}, bf16[16,128,512]{2,1,0:T(8,128)(2,1)}, u32[]{:S(2)}) %copy-start) | copy-done | bytes 2097176
  3.1 0.0 copy-start.1
  3.1 1.0 copy-done.1
  4.1 0.0 copy-start.2
  4.1 0.9 copy-done.2
  5.1 0.0 copy-start.3
  5.1 0.9 copy-done.3
  6.0 0.0 copy-start.4
  6.0 0.8 copy-done.4
  6.8 105.5 %covariance.1 = (f32[128,512]{1,0:T(8,128)S(1)}, f32[128,512]{1,0:T(8,128)S(1)}) custom-call(bf16[16,128,512]{2,1,0:T(8,128)(2,1)S(1)} %copy-done, f32[128,512]{1,0:T(8,128)S(1)} %copy-done.2, f32[128,512]{1,0:T(8,128)S(1)} %copy-done.3, bf16[128,128]{1,0:T(8,128)(2,1)S(1)} %copy-done.4, bf16[12,128,128]{2,1,0:T(8,128)(2,1)S(1)} %copy-done.1, ...), custom_call_target="tpu_custom_call" | custom-call | tf_op jit(solution)/shard_map/covariance/pallas_call | solution.py:291
  112.3 0.7 copy.11
  113.0 0.7 copy.12
Async XLA Ops:
  1.5 1.6 %copy-start = (bf16[16,128,512]{2,1,0:T(8,128)(2,1)S(1)}, bf16[16,128,512]{2,1,0:T(8,128)(2,1)}, u32[]{:S(2)}) copy-start(bf16[16,128,512]{2,1,0:T(8,128)(2,1)} %ens_hbm.1) | copy-start | bytes 6291460
  3.1 1.0 copy-start.1
  4.1 0.9 copy-start.2
  5.1 0.9 copy-start.3
  6.0 0.8 copy-start.4

commit v2 on v0

v2 whole, which is shorter than its diff:
```python
import jax
import jax.numpy as jnp
from jax import lax
from jax.experimental import pallas as pl
from jax.experimental.pallas import tpu as pltpu
from jax.sharding import PartitionSpec as P

MESH = pl.DeviceIdType.MESH
BF = jnp.bfloat16
F32 = jnp.float32

SPREAD = (
    (0, 3, 0), (0, 1, 0), (1, 1, 1), (0, 3, 1), (1, 2, 1), (1, 3, 0), (1, 0, 0), (1, 0, 1),
    (0, 2, 1), (1, 2, 0), (1, 3, 1), (0, 1, 1), (0, 2, 0), (1, 1, 0), (0, 0, 1),
)
ORDER = (2, 1, 3, 0)
BACK = (2, 3, 1, 0)


def device(zhi, x, core, zlo, y):
    return ((zhi * 4 + x) * 2 + core, zlo * 4 + y)


def remote(src, dst, send, recv, to):
    return pltpu.make_async_remote_copy(
        src_ref=src, dst_ref=dst, send_sem=send, recv_sem=recv, device_id=to, device_id_type=MESH)


def kernel(
    ens_hbm, inc_hbm, obs_hbm, vert_hbm, table_hbm, cols_ref,
    out_ref,
    arrived, ens, vl, tcat, vert, inc, obs,
    f1, f2, xo1, xo2, xi1, xi2, r1, r2, q1, q2, s1, s2, w1, w2, last,
    local_sem, es_sem, er_sem,
    gs1, gr1, gs2, gr2, gs3, gr3, hs1, hr1, hs2, hr2, hs3, hr3,
    cs, cr, as_, ar, bs, br, ls, lr,
):
    p, g = lax.axis_index("pts"), lax.axis_index("mem")
    zhi, x, core = p // 8, (p // 2) % 4, p % 2
    zlo, y = g // 4, g % 4
    zz = zhi * 2 + zlo
    other = 1 - core
    partner = device(zhi, x, other, zlo, y)
    flat = other
    a, b = flat * y + core * x, flat * x + core * y
    half = pl.ds(pl.multiple_of(zlo * 64, 64), 64)

    def ring_peer(a2):
        return device(zhi, flat * x + core * a2, core, zlo, flat * a2 + core * y)

    def plane_peer(b2, z2):
        return device(z2 // 2, flat * b2 + core * x, core, z2 % 2, flat * y + core * b2)

    def landed(ref, sem):
        remote(ref, ref, es_sem.at[0], sem, partner).wait_recv()

    def block_of(core2, a2, b2, zh):
        return ((zh * 4 + (1 - core2) * b2 + core2 * a2) * 2 + core2) * 4 + (1 - core2) * a2 + core2 * b2

    mine = pl.ds(pl.multiple_of(y * 128, 128), 128)
    local = [
        pltpu.make_async_copy(inc_hbm.at[:, mine], inc, local_sem.at[0]),
        pltpu.make_async_copy(obs_hbm.at[:, mine], obs, local_sem.at[1]),
        pltpu.make_async_copy(ens_hbm.at[p], arrived.at[p], local_sem.at[2]),
        pltpu.make_async_copy(vert_hbm, vert, local_sem.at[3]),
    ]
    for s in range(12):
        local.append(pltpu.make_async_copy(
            table_hbm.at[s], tcat.at[:, pl.ds(s * 128, 128)], local_sem.at[4 + s]))
    for copy in local:
        copy.start()

    spread_to = [
        device((zhi + dz) % 2, (x + dx) % 4, (core + dc) % 2, zlo, y) for dz, dx, dc in SPREAD
    ]
    mem_peers = [(p, (g + d) % 8) for d in range(1, 8)]
    far = [
        device(flat * ((zhi + k // 4) % 2) + core * (1 - zhi), flat * ((x + k % 4) % 4) + core * x, core,
               flat * (1 - zlo) + core * ((zlo + k // 4) % 2), flat * y + core * ((y + k % 4) % 4))
        for k in range(1, 8)
    ]
    barrier = pltpu.get_barrier_semaphore()
    greet = spread_to + mem_peers + far
    for to in greet:
        pl.semaphore_signal(barrier, inc=1, device_id=to, device_id_type=MESH)

    sent = []
    local[0].wait()
    f1[core, y, x, zhi] = inc[...].T.astype(BF)

    def share(k):
        own = f1.at[core, y, x, zhi]
        copy = remote(own, own, gs1.at[k], gr1.at[zhi * 4 + x],
                      device((zhi + k // 4) % 2, (x + k % 4) % 4, core, zlo, y))
        copy.start()
        sent.append(copy)

    def spread(k):
        to = spread_to[k]
        copy = remote(ens_hbm.at[to[0]], arrived.at[p], es_sem.at[k], er_sem.at[p], to)
        copy.start()
        sent.append(copy)

    pl.semaphore_wait(barrier, len(greet))
    for k in (1, 3, 4, 2, 5, 7, 6):
        share(k)
    for k in range(15):
        spread(k)
    for k in range(1, 8):
        x2, zh = (x + k % 4) % 4, (zhi + k // 4) % 2
        landed(f1.at[core, y, x2, zh], gr1.at[zh * 4 + x2])
    own = f1.at[core, y]
    for d in (1, 2, 3):
        copy = remote(own, own, gs2.at[d], gr2.at[y], device(zhi, x, core, zlo, (y + d) % 4))
        copy.start()
        sent.append(copy)
    for d in range(4):
        slot = f1.at[core, (y + d) % 4]
        if d:
            landed(slot, gr2.at[(y + d) % 4])
        copy = remote(slot, slot, gs3.at[d], gr3.at[(y + d) % 4], partner)
        copy.start()
        sent.append(copy)
    for d in range(4):
        landed(f1.at[other, (y + d) % 4], gr3.at[(y + d) % 4])

    def mix(product):
        return lax.dot_general(product.astype(BF), vert[...], (((1,), (1,)), ((), ())),
                               preferred_element_type=F32).astype(BF)

    local[3].wait()
    for k in range(16):
        dz, dx, dc = (0, 0, 0) if k == 0 else SPREAD[k - 1]
        zh, x2, core2 = (zhi + dz) % 2, (x + 4 - dx) % 4, (core + dc) % 2
        p2 = (zh * 4 + x2) * 2 + core2
        if k == 0:
            local[2].wait()
        else:
            landed(arrived.at[p2], er_sem.at[p2])
        products = []
        for yy in range(4):
            share = arrived[p2, :, yy * 128:(yy + 1) * 128].T
            ens[p2 * 4 + yy] = share
            products.append((share.astype(F32) * f1[core2, yy, x2, zh].astype(F32)).astype(BF))
        mixed = mix(jnp.concatenate(products, axis=0))
        for yy in range(4):
            vl[p2 * 4 + yy] = mixed[yy * 128:(yy + 1) * 128]
    for s in range(12):
        local[4 + s].wait()

    def vertical(f, core2, a2):
        products = []
        blocks = []
        for b2 in range(4):
            for zh in range(2):
                r = block_of(core2, a2, b2, zh)
                blocks.append(r)
                products.append((ens[r].astype(F32) * f[core2, a2, b2, zh].astype(F32)).astype(BF))
        mixed = mix(jnp.concatenate(products, axis=0))
        for k, r in enumerate(blocks):
            vl[r] = mixed[k * 128:(k + 1) * 128]

    def horizontal(core2, a2):
        blocks = [block_of(core2, a2, b2, zh) for b2 in range(4) for zh in range(2)]
        stacked = jnp.concatenate(
            [jnp.concatenate([vl[cols_ref[s, r]] for s in range(12)], axis=0) for r in blocks], axis=1)
        total = jnp.dot(tcat[...], stacked, preferred_element_type=F32).astype(BF)
        return [ens[r].astype(F32) * total[:, k * 128:(k + 1) * 128].astype(F32)
                for k, r in enumerate(blocks)]

    def step_of(t):
        return jnp.where(t == 0, 2, jnp.where(t == 1, 1, jnp.where(t == 2, 3, 0)))

    def scatter(n, xo, xi, r, q, s_buf, w):
        a_other = flat * x + core * y

        def core_copy(t):
            return remote(xo.at[t], xi.at[t], cs.at[n, t], cr.at[n, t], partner)

        def away(t):
            for k, value in enumerate(horizontal(other, (a_other + step_of(t)) % 4)):
                xo[t, k] = value.astype(BF)
            core_copy(t).start()

        def keep(t):
            values = horizontal(core, (a + step_of(t)) % 4)
            core_copy(t).wait_recv()
            for k, value in enumerate(values):
                r[t, k // 2, k % 2] = (value + xi[t, k].astype(F32)).astype(BF)

        def ring_copy(t, b2):
            return remote(r.at[t, b2], q.at[t, b2], as_.at[n, t, b2], ar.at[n, t, b2],
                          ring_peer((a + step_of(t)) % 4))

        def both(t, carry):
            away(t + 1)
            keep(t)
            for d in ORDER:
                ring_copy(t, (b + d) % 4).start()
            return carry

        away(0)
        lax.fori_loop(0, 3, both, 0)
        keep(3)

        def plane_copy(b2, z2):
            rows = pl.ds(pl.multiple_of((z2 % 2) * 64, 64), 64)
            return remote(s_buf.at[b2, z2 // 2, rows], w.at[b * 4 + zz], bs.at[n, b2 * 4 + z2],
                          br.at[n, b * 4 + zz], plane_peer(b2, z2))

        plane = []
        for d in ORDER:
            b2 = (b + d) % 4
            total = r[3, b2].astype(F32)
            for t in range(3):
                landed(q.at[t, b2], ar.at[n, t, b2])
                total = total + q[t, b2].astype(F32)
            s_buf[b2] = total.astype(BF)
            for dz in ORDER:
                if d or dz:
                    copy = plane_copy(b2, (zz + dz) % 4)
                    copy.start()
                    plane.append(copy)
        total = s_buf[b, zhi, half].astype(F32)
        for d in BACK:
            for dz in BACK:
                if d or dz:
                    k = (b + d) % 4 * 4 + (zz + dz) % 4
                    landed(w.at[k], br.at[n, k])
                    total = total + w[k].astype(F32)

        def finish():
            for t in range(4):
                core_copy(t).wait_send()
            for t in range(3):
                for b2 in range(4):
                    ring_copy(t, b2).wait_send()
            for copy in plane:
                copy.wait_send()

        return total, finish

    first, finish1 = scatter(0, xo1, xi1, r1, q1, s1, w1)

    local[1].wait()
    obs[...] = obs[...].T
    f2[core, a, b, zhi, half] = (first * obs[half]).astype(BF)

    def piece(a2, d, dz):
        b2, z2 = (b + d) % 4, (zz + dz) % 4
        rows = pl.ds(pl.multiple_of((z2 % 2) * 64, 64), 64)
        return f2.at[core, a2, b2, z2 // 2, rows], b2 * 4 + z2

    def pass_on(d, dz):
        slot, k = piece(a, d, dz)
        for da in (2, 1, 3):
            copy = remote(slot, slot, hs2.at[da, k], hr2.at[a, k], ring_peer((a + da) % 4))
            copy.start()
            sent.append(copy)

    pass_on(0, 0)
    own, k = piece(a, 0, 0)
    for d in (0, 1, 3, 2):
        for dz in (2, 1, 3, 0):
            if d or dz:
                copy = remote(own, own, hs1.at[d * 4 + dz], hr1.at[k],
                              plane_peer((b + d) % 4, (zz + dz) % 4))
                copy.start()
                sent.append(copy)
    for d in (0, 3, 1, 2):
        for dz in BACK:
            if d or dz:
                slot, k = piece(a, d, dz)
                landed(slot, hr1.at[k])
                pass_on(d, dz)
    def hand_over(a2, d):
        slot = f2.at[core, a2, (b + d) % 4]
        copy = remote(slot, slot, hs3.at[a2, d], hr3.at[a2, (b + d) % 4], partner)
        copy.start()
        sent.append(copy)

    a_other, b_other = flat * x + core * y, flat * y + core * x
    for d in (0, 3, 1, 2):
        hand_over(a, d)
    vertical(f2, core, a)
    for da in (0, 1, 3, 2):
        a2 = (a + da) % 4
        if da:
            for d in (0, 3, 1, 2):
                for dz in BACK:
                    slot, k = piece(a2, d, dz)
                    landed(slot, hr2.at[a2, k])
                hand_over(a2, d)
            vertical(f2, core, a2)
        a2 = (a_other + da) % 4
        for d in (0, 3, 1, 2):
            b2 = (b_other + d) % 4
            landed(f2.at[other, a2, b2], hr3.at[a2, b2])
        vertical(f2, other, a2)
    second, finish2 = scatter(1, xo2, xi2, r2, q2, s2, w2)

    last[g] = second.astype(BF)
    out = []
    for k, to in enumerate(mem_peers):
        copy = remote(last.at[g], last.at[g], ls.at[k], lr.at[g], to)
        copy.start()
        out.append(copy)
    for yy in range(4):
        block = f2[core, flat * yy + core * x, flat * x + core * yy, zhi]
        out_ref[0, :, yy * 128:(yy + 1) * 128] = block.T
    finish1()
    finish2()
    for copy in sent:
        copy.wait_send()
    for d in range(1, 8):
        k = (g + d) % 8
        landed(last.at[k], lr.at[k])
    for yy in range(4):
        block = jnp.concatenate([last[yy], last[4 + yy]], axis=0)
        out_ref[1, :, yy * 128:(yy + 1) * 128] = block.T
    for copy in out:
        copy.wait_send()


def per_device(ensemble, increment, obs_weight, vertical, block_table, block_cols):
    dma = pltpu.SemaphoreType.DMA
    vmem = pl.BlockSpec(memory_space=pltpu.VMEM)
    hbm = pl.BlockSpec(memory_space=pltpu.HBM)
    twice = lambda shape, kind=BF: [pltpu.VMEM(shape, kind)] * 2
    both = pl.pallas_call(
        kernel,
        out_shape=jax.ShapeDtypeStruct((2, 128, 512), BF),
        in_specs=[hbm, hbm, hbm, hbm, hbm, pl.BlockSpec(memory_space=pltpu.SMEM)],
        out_specs=vmem,
        scratch_shapes=[
            pltpu.VMEM((16, 128, 512), BF),
            pltpu.VMEM((64, 128, 128), BF),
            pltpu.VMEM((64, 128, 128), BF),
            pltpu.VMEM((128, 12 * 128), BF),
            pltpu.VMEM((128, 128), BF),
            pltpu.VMEM((128, 128), F32),
            pltpu.VMEM((128, 128), F32),
        ] + twice((2, 4, 4, 2, 128, 128)) + twice((4, 8, 128, 128)) + twice((4, 8, 128, 128))
        + twice((4, 4, 2, 128, 128)) + twice((3, 4, 2, 128, 128)) + twice((4, 2, 128, 128))
        + twice((16, 64, 128))
        + [
            pltpu.VMEM((8, 64, 128), BF),
            dma((16,)), dma((15,)), dma((16,)),
            dma((8,)), dma((8,)), dma((4,)), dma((4,)), dma((4,)), dma((4,)),
            dma((16,)), dma((16,)), dma((4, 16)), dma((4, 16)), dma((4, 4)), dma((4, 4)),
            dma((2, 4)), dma((2, 4)), dma((2, 3, 4)), dma((2, 3, 4)), dma((2, 16)), dma((2, 16)),
            dma((7,)), dma((8,)),
        ],
        compiler_params=pltpu.CompilerParams(
            collective_id=0, has_side_effects=True, vmem_limit_bytes=62 * 1024 * 1024),
        name="covariance",
    )(ensemble, increment, obs_weight, vertical, block_table, block_cols.T)
    return both[0].astype(F32), both[1].astype(F32)


def solution(mesh):
    return jax.shard_map(
        per_device,
        mesh=mesh,
        in_specs=(P("mem", None, "pts"), P(None, "pts"), P(None, "pts"), P(), P(), P()),
        out_specs=(P(None, "pts"), P(None, "pts")),
        check_vma=False,
    )
```

time: 434 us -> 96.1 us (0.22)
  matrix products: 119 us -> 0 us
  local copies, waits for them, and re-layouts: 109 us -> 0 us
  Pallas kernels: 0 us -> 92 us
  blocking collectives: 91.5 us -> 0 us
  waiting for transfers between devices: 49.6 us -> 0 us
  other arithmetic: 37 us -> 1.82 us
  starting transfers between devices: 21.3 us -> 0 us
    dot_general x26 -> x0, matrix products: 119 us -> none  [the longest x24 115 us: add_slot(): jnp.einsum('rnk,lk->rnl', picked, kernel, preferred_element_type=jnp.floa...]
    pallas_call x0 -> x1, Pallas kernels: none -> 92 us  [per_device(): pl.pallas_call(kernel, out_shape=jax.ShapeDtypeStruct((2, 128, 512), BF),...]
    all_to_all x4 -> x0, blocking collectives: 91.5 us -> none  [the longest x2 62.8 us: sent_to_all(): return lax.all_to_all(copies, axis, split_axis=0, concat_axis=0, tiled=True)]
    gather x24 -> x0, local copies, waits for them, and re-layouts: 61 us -> none  [add_slot(): picked = jnp.take(flattened, chosen, axis=1)]
    all_to_all x3 -> x0, waiting for transfers between devices: 49.6 us -> none  [the longest x2 49.6 us: cov_local(): lax.all_to_all(vert_mixed, 'pts', split_axis=1, concat_axis=2, tiled=True)]
    convert_element_type x6 -> x0, local copies, waits for them, and re-layouts: 26.2 us -> none  [the longest x4 18.6 us: cov_local(): level_local.astype(jnp.float32)]
    all_to_all x3 -> x0, starting transfers between devices: 21.3 us -> none  [the longest x2 13.5 us: cov_local(): lax.all_to_all(vert_mixed, 'pts', split_axis=1, concat_axis=2, tiled=True)]
    and x24 -> x0, other arithmetic: 16.7 us -> none  [add_slot(): picked = jnp.take(flattened, chosen, axis=1)]
  transfers between devices with their start and end apart: 3 -> 0, of which waited for: 2 -> 0; matrix products, arithmetic and copies ran while one was open for 28% -> 0% of each run, Pallas kernels for 0% -> 0%
where the time goes in v2:
time: 96.1 us; the launch traced here: 94.5 us
  Pallas kernels  92 us (96%)
  other arithmetic  1.82 us (2%)
    pallas_call x1, Pallas kernels, per_device(): pl.pallas_call(kernel, out_shape=jax.ShapeDtypeStruct((2, 128, 512), BF),...  92 us

profile of v2, /device:TPU:6, one launch (start us, length us, event | category | flops | bytes accessed | tf_op | source)
XLA Modules:
  0.0 94.5 jit_solution(14534977788317749298)
XLA Ops:
  0.6 92.0 %covariance.1 = bf16[2,128,512]{2,1,0:T(8,128)(2,1)} custom-call(bf16[16,128,512]{2,1,0:T(8,128)(2,1)} %ens_hbm.1, f32[128,512]{1,0:T(8,128)} %inc_hbm.1, f32[128,512]{1,0:T(8,128)} %obs_hbm.1, bf16[128,128]{1,0:T(8,128)(2,1)} %vert_hbm.1, bf16[12,128,128]{2,1,0:T(8,128)(2,1)} %table_hbm.1, s32[12,64]{1,0:T(8,128)} %bitcast.7), custom_call_target="tpu_custom_call" | custom-call | tf_op jit(solution)/shard_map/covariance/pallas_call | solution.py:330
  92.7 1.8 %bitcast_convert_fusion = (f32[128,512]{1,0:T(8,128)}, f32[128,512]{1,0:T(8,128)}) fusion(bf16[2,128,512]{2,1,0:T(8,128)(2,1)} %covariance.1), kind=kLoop, calls=%fused_computation | loop fusion | flops 131072 | bytes 786432 | tf_op jit(solution)/shard_map/convert_element_type | solution.py:358

commit v3 on v2

v3 whole, which is shorter than its diff:
```python
import jax
import jax.numpy as jnp
from jax import lax
from jax.experimental import pallas as pl
from jax.experimental.pallas import tpu as pltpu
from jax.sharding import PartitionSpec as P

MESH = pl.DeviceIdType.MESH
BF = jnp.bfloat16
F32 = jnp.float32

SPREAD = (
    (0, 3, 0), (0, 1, 0), (1, 1, 1), (0, 3, 1), (1, 2, 1), (1, 3, 0), (1, 0, 0), (1, 0, 1),
    (0, 2, 1), (1, 2, 0), (1, 3, 1), (0, 1, 1), (0, 2, 0), (1, 1, 0), (0, 0, 1),
)
ORDER = (2, 1, 3, 0)
BACK = (2, 3, 1, 0)


def device(zhi, x, core, zlo, y):
    return ((zhi * 4 + x) * 2 + core, zlo * 4 + y)


def remote(src, dst, send, recv, to):
    return pltpu.make_async_remote_copy(
        src_ref=src, dst_ref=dst, send_sem=send, recv_sem=recv, device_id=to, device_id_type=MESH)


def kernel(
    ens_hbm, inc_hbm, obs_hbm, vert_hbm, table_hbm, cols_hbm,
    out_ref,
    cols_ref, arrived, ens, vl, tcat, vert, inc, obs,
    f1, f2, xo1, xo2, xi1, xi2, r1, r2, q1, q2, s1, s2, w1, w2, last,
    local_sem, es_sem, er_sem,
    gs1, gr1, gs2, gr2, gs3, gr3, hs1, hr1, hs2, hr2, hs3, hr3,
    cs, cr, as_, ar, bs, br, ls, lr,
):
    p, g = lax.axis_index("pts"), lax.axis_index("mem")
    zhi, x, core = p // 8, (p // 2) % 4, p % 2
    zlo, y = g // 4, g % 4
    zz = zhi * 2 + zlo
    other = 1 - core
    partner = device(zhi, x, other, zlo, y)
    flat = other
    a, b = flat * y + core * x, flat * x + core * y
    half = pl.ds(pl.multiple_of(zlo * 64, 64), 64)

    def ring_peer(a2):
        return device(zhi, flat * x + core * a2, core, zlo, flat * a2 + core * y)

    def plane_peer(b2, z2):
        return device(z2 // 2, flat * b2 + core * x, core, z2 % 2, flat * y + core * b2)

    def landed(ref, sem):
        remote(ref, ref, es_sem, sem, partner).wait_recv()

    def drained(ref, sem):
        remote(ref, ref, sem, er_sem.at[0], partner).wait_send()

    def blocks(n):
        return ens.at[pl.ds(0, n)]

    def pieces(n):
        return w1.at[pl.ds(0, n)]

    def block_of(core2, a2, b2, zh):
        return ((zh * 4 + (1 - core2) * b2 + core2 * a2) * 2 + core2) * 4 + (1 - core2) * a2 + core2 * b2

    mine = pl.ds(pl.multiple_of(y * 128, 128), 128)
    local = [
        pltpu.make_async_copy(inc_hbm.at[:, mine], inc, local_sem.at[0]),
        pltpu.make_async_copy(obs_hbm.at[:, mine], obs, local_sem.at[1]),
        pltpu.make_async_copy(ens_hbm.at[p], arrived.at[p], local_sem.at[2]),
        pltpu.make_async_copy(vert_hbm, vert, local_sem.at[3]),
    ]
    for s in range(12):
        local.append(pltpu.make_async_copy(
            table_hbm.at[s], tcat.at[:, pl.ds(s * 128, 128)], local_sem.at[4]))
    local.append(pltpu.make_async_copy(cols_hbm, cols_ref, local_sem.at[5]))
    for copy in local:
        copy.start()

    spread_to = [
        device((zhi + dz) % 2, (x + dx) % 4, (core + dc) % 2, zlo, y) for dz, dx, dc in SPREAD
    ]
    mem_peers = [(p, (g + d) % 8) for d in range(1, 8)]
    far = [
        device(flat * ((zhi + k // 4) % 2) + core * (1 - zhi), flat * ((x + k % 4) % 4) + core * x, core,
               flat * (1 - zlo) + core * ((zlo + k // 4) % 2), flat * y + core * ((y + k % 4) % 4))
        for k in range(1, 8)
    ]
    barrier = pltpu.get_barrier_semaphore()
    greet = spread_to + mem_peers + far
    for to in greet:
        pl.semaphore_signal(barrier, inc=1, device_id=to, device_id_type=MESH)

    local[0].wait()
    f1[core, y, x, zhi] = inc[...].T.astype(BF)

    def share(k):
        own = f1.at[core, y, x, zhi]
        copy = remote(own, own, gs1, gr1,
                      device((zhi + k // 4) % 2, (x + k % 4) % 4, core, zlo, y))
        copy.start()

    def spread(k):
        to = spread_to[k]
        copy = remote(ens_hbm.at[to[0]], arrived.at[p], es_sem, er_sem.at[p], to)
        copy.start()

    pl.semaphore_wait(barrier, len(greet))
    for k in (1, 3, 4, 2, 5, 7, 6):
        share(k)
    for k in range(15):
        spread(k)
    landed(blocks(7), gr1)
    own = f1.at[core, y]
    for d in (1, 2, 3):
        remote(own, own, gs2, gr2, device(zhi, x, core, zlo, (y + d) % 4)).start()
    landed(blocks(24), gr2)
    own = f1.at[core]
    remote(own, own, gs3, gr3, partner).start()
    landed(blocks(32), gr3)

    def mix(product):
        return lax.dot_general(product.astype(BF), vert[...], (((1,), (1,)), ((), ())),
                               preferred_element_type=F32).astype(BF)

    local[3].wait()
    for k in range(16):
        dz, dx, dc = (0, 0, 0) if k == 0 else SPREAD[k - 1]
        zh, x2, core2 = (zhi + dz) % 2, (x + 4 - dx) % 4, (core + dc) % 2
        p2 = (zh * 4 + x2) * 2 + core2
        if k == 0:
            local[2].wait()
        else:
            landed(arrived.at[p2], er_sem.at[p2])
        products = []
        for yy in range(4):
            share = arrived[p2, :, yy * 128:(yy + 1) * 128].T
            ens[p2 * 4 + yy] = share
            products.append((share.astype(F32) * f1[core2, yy, x2, zh].astype(F32)).astype(BF))
        mixed = mix(jnp.concatenate(products, axis=0))
        for yy in range(4):
            vl[p2 * 4 + yy] = mixed[yy * 128:(yy + 1) * 128]
    pltpu.make_async_copy(tcat, tcat, local_sem.at[4]).wait()
    local[-1].wait()

    def vertical(f, core2, a2):
        products = []
        blocks = []
        for b2 in range(4):
            for zh in range(2):
                r = block_of(core2, a2, b2, zh)
                blocks.append(r)
                products.append((ens[r].astype(F32) * f[core2, a2, b2, zh].astype(F32)).astype(BF))
        mixed = mix(jnp.concatenate(products, axis=0))
        for k, r in enumerate(blocks):
            vl[r] = mixed[k * 128:(k + 1) * 128]

    def horizontal(core2, a2):
        blocks = [block_of(core2, a2, b2, zh) for b2 in range(4) for zh in range(2)]
        stacked = jnp.concatenate(
            [jnp.concatenate([vl[cols_ref[s, r]] for s in range(12)], axis=0) for r in blocks], axis=1)
        total = jnp.dot(tcat[...], stacked, preferred_element_type=F32).astype(BF)
        return [ens[r].astype(F32) * total[:, k * 128:(k + 1) * 128].astype(F32)
                for k, r in enumerate(blocks)]

    def step_of(t):
        return jnp.where(t == 0, 2, jnp.where(t == 1, 1, jnp.where(t == 2, 3, 0)))

    def scatter(n, xo, xi, r, q, s_buf, w):
        a_other = flat * x + core * y

        def core_copy(t):
            return remote(xo.at[t], xi.at[t], cs.at[n], cr.at[n, t], partner)

        def away(t):
            for k, value in enumerate(horizontal(other, (a_other + step_of(t)) % 4)):
                xo[t, k] = value.astype(BF)
            core_copy(t).start()

        def keep(t):
            values = horizontal(core, (a + step_of(t)) % 4)
            core_copy(t).wait_recv()
            for k, value in enumerate(values):
                r[t, k // 2, k % 2] = (value + xi[t, k].astype(F32)).astype(BF)

        def ring_copy(t, b2):
            return remote(r.at[t, b2], q.at[t, b2], as_.at[n], ar.at[n, b2],
                          ring_peer((a + step_of(t)) % 4))

        def both(t, carry):
            away(t + 1)
            keep(t)
            for d in ORDER:
                ring_copy(t, (b + d) % 4).start()
            return carry

        away(0)
        lax.fori_loop(0, 3, both, 0)
        keep(3)

        def plane_copy(b2, z2):
            rows = pl.ds(pl.multiple_of((z2 % 2) * 64, 64), 64)
            return remote(s_buf.at[b2, z2 // 2, rows], w.at[b * 4 + zz], bs.at[n],
                          br.at[n], plane_peer(b2, z2))

        for d in ORDER:
            b2 = (b + d) % 4
            total = r[3, b2].astype(F32)
            landed(blocks(6), ar.at[n, b2])
            for t in range(3):
                total = total + q[t, b2].astype(F32)
            s_buf[b2] = total.astype(BF)
            for dz in ORDER:
                if d or dz:
                    plane_copy(b2, (zz + dz) % 4).start()
        total = s_buf[b, zhi, half].astype(F32)
        landed(pieces(15), br.at[n])
        for d in BACK:
            for dz in BACK:
                if d or dz:
                    k = (b + d) % 4 * 4 + (zz + dz) % 4
                    total = total + w[k].astype(F32)

        return total

    first = scatter(0, xo1, xi1, r1, q1, s1, w1)

    local[1].wait()
    obs[...] = obs[...].T
    f2[core, a, b, zhi, half] = (first * obs[half]).astype(BF)

    own = f2.at[core, a, b, zhi, half]
    for d in (0, 1, 3, 2):
        for dz in (2, 1, 3, 0):
            if d or dz:
                remote(own, own, hs1, hr1.at[b], plane_peer((b + d) % 4, (zz + dz) % 4)).start()
    for d in (0, 3, 1, 2):
        b2 = (b + d) % 4
        landed(pieces(4 if d else 3), hr1.at[b2])
        slot = f2.at[core, a, b2]
        for da in (2, 1, 3):
            remote(slot, slot, hs2, hr2.at[a, b2], ring_peer((a + da) % 4)).start()

    def hand_over(a2):
        slot = f2.at[core, a2]
        remote(slot, slot, hs3, hr3.at[a2], partner).start()

    hand_over(a)
    vertical(f2, core, a)
    for da in (0, 1, 3, 2):
        a2 = (a + da) % 4
        if da:
            for d in (0, 3, 1, 2):
                landed(blocks(2), hr2.at[a2, (b + d) % 4])
            hand_over(a2)
            vertical(f2, core, a2)
        a2 = (flat * x + core * y + da) % 4
        landed(blocks(8), hr3.at[a2])
        vertical(f2, other, a2)
    second = scatter(1, xo2, xi2, r2, q2, s2, w2)

    last[g] = second.astype(BF)
    for to in mem_peers:
        remote(last.at[g], last.at[g], ls, lr, to).start()
    for yy in range(4):
        block = f2[core, flat * yy + core * x, flat * x + core * yy, zhi]
        out_ref[0, :, yy * 128:(yy + 1) * 128] = block.T
    drained(arrived.at[pl.ds(0, 15)], es_sem)
    drained(blocks(7), gs1)
    drained(blocks(24), gs2)
    drained(blocks(32), gs3)
    drained(pieces(15), hs1)
    drained(blocks(24), hs2)
    drained(blocks(32), hs3)
    for n in range(2):
        drained(blocks(32), cs.at[n])
        drained(blocks(24), as_.at[n])
        drained(pieces(15), bs.at[n])
    landed(pieces(7), lr)
    for yy in range(4):
        block = jnp.concatenate([last[yy], last[4 + yy]], axis=0)
        out_ref[1, :, yy * 128:(yy + 1) * 128] = block.T
    drained(pieces(7), ls)


def per_device(ensemble, increment, obs_weight, vertical, block_table, block_cols):
    dma = pltpu.SemaphoreType.DMA
    vmem = pl.BlockSpec(memory_space=pltpu.VMEM)
    hbm = pl.BlockSpec(memory_space=pltpu.HBM)
    twice = lambda shape, kind=BF: [pltpu.VMEM(shape, kind)] * 2
    both = pl.pallas_call(
        kernel,
        out_shape=jax.ShapeDtypeStruct((2, 128, 512), BF),
        in_specs=[hbm] * 6,
        out_specs=vmem,
        scratch_shapes=[
            pltpu.SMEM((12, 64), jnp.int32),
            pltpu.VMEM((16, 128, 512), BF),
            pltpu.VMEM((64, 128, 128), BF),
            pltpu.VMEM((64, 128, 128), BF),
            pltpu.VMEM((128, 12 * 128), BF),
            pltpu.VMEM((128, 128), BF),
            pltpu.VMEM((128, 128), F32),
            pltpu.VMEM((128, 128), F32),
        ] + twice((2, 4, 4, 2, 128, 128)) + twice((4, 8, 128, 128)) + twice((4, 8, 128, 128))
        + twice((4, 4, 2, 128, 128)) + twice((3, 4, 2, 128, 128)) + twice((4, 2, 128, 128))
        + twice((16, 64, 128))
        + [
            pltpu.VMEM((8, 64, 128), BF),
            dma((6,)), dma, dma((16,)),
            dma, dma, dma, dma, dma, dma, dma, dma((4,)), dma, dma((4, 4)), dma, dma((4,)),
            dma((2,)), dma((2, 4)), dma((2,)), dma((2, 4)), dma((2,)), dma((2,)), dma, dma,
        ],
        compiler_params=pltpu.CompilerParams(
            collective_id=0, has_side_effects=True, vmem_limit_bytes=48 * 1024 * 1024),
        name="covariance",
    )(*[pltpu.with_memory_space_constraint(v, pltpu.HBM) for v in (ensemble, increment, obs_weight, vertical, block_table, block_cols.T)])
    return both[0].astype(F32), both[1].astype(F32)


def solution(mesh):
    return jax.shard_map(
        per_device,
        mesh=mesh,
        in_specs=(P("mem", None, "pts"), P(None, "pts"), P(None, "pts"), P(), P(), P()),
        out_specs=(P(None, "pts"), P(None, "pts")),
        check_vma=False,
    )
```

time: 96.1 us -> 91.7 us (0.954)
  Pallas kernels: 92 us -> 88.7 us
  other arithmetic: 1.82 us -> 0.85 us
    pallas_call x1, Pallas kernels: 92 us -> 88.7 us  [per_device(): pl.pallas_call(kernel, out_shape=jax.ShapeDtypeStruct((2, 128, 512), BF),...]
    convert_element_type x1, other arithmetic: 1.82 us -> 0.85 us  [per_device(): return (both[0].astype(F32), both[1].astype(F32))]
where the time goes in v3:
time: 91.7 us; the launch traced here: 90.2 us
  Pallas kernels  88.7 us (97%)
    pallas_call x1, Pallas kernels, per_device(): pl.pallas_call(kernel, out_shape=jax.ShapeDtypeStruct((2, 128, 512), BF),...  88.7 us

profile of v3, /device:TPU:6, one launch (start us, length us, event | category | flops | bytes accessed | tf_op | source)
XLA Modules:
  0.0 90.2 jit_solution(12118926346873368538)
XLA Ops:
  0.6 88.7 %covariance.1 = bf16[2,128,512]{2,1,0:T(8,128)(2,1)S(1)} custom-call(bf16[16,128,512]{2,1,0:T(8,128)(2,1)} %ens_hbm.1, f32[128,512]{1,0:T(8,128)} %inc_hbm.1, f32[128,512]{1,0:T(8,128)} %obs_hbm.1, bf16[128,128]{1,0:T(8,128)(2,1)} %vert_hbm.1, bf16[12,128,128]{2,1,0:T(8,128)(2,1)} %table_hbm.1, s32[12,64]{1,0:T(8,128)} %bitcast.7), custom_call_target="tpu_custom_call" | custom-call | tf_op jit(solution)/shard_map/covariance/pallas_call | solution.py:294
  89.3 0.9 bitcast_convert_fusion

commit v4 on v3

--- a/solution.py
+++ b/solution.py
@@ -126,6 +126,8 @@
         return lax.dot_general(product.astype(BF), vert[...], (((1,), (1,)), ((), ())),
                                preferred_element_type=F32).astype(BF)
 
+    local[1].wait()
+    obs[...] = obs[...].T
     local[3].wait()
     for k in range(16):
         dz, dx, dc = (0, 0, 0) if k == 0 else SPREAD[k - 1]
@@ -228,38 +230,53 @@
 
     first = scatter(0, xo1, xi1, r1, q1, s1, w1)
 
-    local[1].wait()
-    obs[...] = obs[...].T
     f2[core, a, b, zhi, half] = (first * obs[half]).astype(BF)
 
-    own = f2.at[core, a, b, zhi, half]
+    def piece(d, dz):
+        b2, z2 = (b + d) % 4, (zz + dz) % 4
+        rows = pl.ds(pl.multiple_of((z2 % 2) * 64, 64), 64)
+        return f2.at[core, a, b2, z2 // 2, rows], b2
+
+    def pass_on(d, dz):
+        slot, b2 = piece(d, dz)
+        for da in (1, 3, 2):
+            remote(slot, slot, hs2, hr2.at[a, b2], ring_peer((a + da) % 4)).start()
+
+    pass_on(0, 0)
+    own, b2 = piece(0, 0)
     for d in (0, 1, 3, 2):
         for dz in (2, 1, 3, 0):
             if d or dz:
-                remote(own, own, hs1, hr1.at[b], plane_peer((b + d) % 4, (zz + dz) % 4)).start()
+                remote(own, own, hs1, hr1.at[b * 4 + zz], plane_peer((b + d) % 4, (zz + dz) % 4)).start()
     for d in (0, 3, 1, 2):
-        b2 = (b + d) % 4
-        landed(pieces(4 if d else 3), hr1.at[b2])
-        slot = f2.at[core, a, b2]
-        for da in (2, 1, 3):
-            remote(slot, slot, hs2, hr2.at[a, b2], ring_peer((a + da) % 4)).start()
+        for dz in (0, 1, 3, 2):
+            if d or dz:
+                landed(pieces(1), hr1.at[(b + d) % 4 * 4 + (zz + dz) % 4])
+                pass_on(d, dz)
 
     def hand_over(a2):
         slot = f2.at[core, a2]
         remote(slot, slot, hs3, hr3.at[a2], partner).start()
 
-    hand_over(a)
-    vertical(f2, core, a)
-    for da in (0, 1, 3, 2):
-        a2 = (a + da) % 4
-        if da:
-            for d in (0, 3, 1, 2):
-                landed(blocks(2), hr2.at[a2, (b + d) % 4])
-            hand_over(a2)
-            vertical(f2, core, a2)
+    def take(da):
         a2 = (flat * x + core * y + da) % 4
         landed(blocks(8), hr3.at[a2])
         vertical(f2, other, a2)
+
+    hand_over(a)
+    vertical(f2, core, a)
+    before = 0
+    for da in (1, 3, 2):
+        a2 = (a + da) % 4
+        for d in (0, 3, 1, 2):
+            b2 = (b + d) % 4
+            landed(blocks(2), hr2.at[a2, b2])
+            slot = f2.at[core, a2, b2]
+            remote(slot, slot, hs3, hr3.at[a2], partner).start()
+        vertical(f2, core, a2)
+        take(before)
+        before = da
+    take(2)
     second = scatter(1, xo2, xi2, r2, q2, s2, w2)
 
     last[g] = second.astype(BF)
@@ -311,7 +328,7 @@
         + [
             pltpu.VMEM((8, 64, 128), BF),
             dma((6,)), dma, dma((16,)),
-            dma, dma, dma, dma, dma, dma, dma, dma((4,)), dma, dma((4, 4)), dma, dma((4,)),
+            dma, dma, dma, dma, dma, dma, dma, dma((16,)), dma, dma((4, 4)), dma, dma((4,)),
             dma((2,)), dma((2, 4)), dma((2,)), dma((2, 4)), dma((2,)), dma((2,)), dma, dma,
         ],
         compiler_params=pltpu.CompilerParams(

time: 91.7 us -> 89.2 us (0.973)
  Pallas kernels: 88.7 us -> 86.3 us
    pallas_call x1, Pallas kernels: 88.7 us -> 86.3 us  [per_device(): pl.pallas_call(kernel, out_shape=jax.ShapeDtypeStruct((2, 128, 512), BF),...]
where the time goes in v4:
time: 89.2 us; the launch traced here: 87.8 us
  Pallas kernels  86.3 us (97%)
    pallas_call x1, Pallas kernels, per_device(): pl.pallas_call(kernel, out_shape=jax.ShapeDtypeStruct((2, 128, 512), BF),...  86.3 us

profile of v4, /device:TPU:6, one launch (start us, length us, event | category | flops | bytes accessed | tf_op | source)
XLA Modules:
  0.0 87.8 jit_solution(13663894425403964235)
XLA Ops:
  0.6 86.3 %covariance.1 = bf16[2,128,512]{2,1,0:T(8,128)(2,1)S(1)} custom-call(bf16[16,128,512]{2,1,0:T(8,128)(2,1)} %ens_hbm.1, f32[128,512]{1,0:T(8,128)} %inc_hbm.1, f32[128,512]{1,0:T(8,128)} %obs_hbm.1, bf16[128,128]{1,0:T(8,128)(2,1)} %vert_hbm.1, bf16[12,128,128]{2,1,0:T(8,128)(2,1)} %table_hbm.1, s32[12,64]{1,0:T(8,128)} %bitcast.7), custom_call_target="tpu_custom_call" | custom-call | tf_op jit(solution)/shard_map/covariance/pallas_call | solution.py:311
  86.9 0.9 bitcast_convert_fusion

commit v5 on v4

--- a/solution.py
+++ b/solution.py
@@ -83,7 +83,8 @@
     spread_to = [
         device((zhi + dz) % 2, (x + dx) % 4, (core + dc) % 2, zlo, y) for dz, dx, dc in SPREAD
     ]
-    mem_peers = [(p, (g + d) % 8) for d in range(1, 8)]
+    mem_peers = [(p, (zlo + dz) % 2 * 4 + (y + dy) % 4)
+                 for dz, dy in ((1, 2), (1, 1), (1, 3), (0, 2), (0, 1), (0, 3), (1, 0))]
     far = [
         device(flat * ((zhi + k // 4) % 2) + core * (1 - zhi), flat * ((x + k % 4) % 4) + core * x, core,
                flat * (1 - zlo) + core * ((zlo + k // 4) % 2), flat * y + core * ((y + k % 4) % 4))

time: 89.2 us -> 89.1 us (level)
  no operation moved by 1% of the time
where the time goes in v5:
time: 89.1 us; the launch traced here: 87.7 us
  Pallas kernels  86.3 us (97%)
    pallas_call x1, Pallas kernels, per_device(): pl.pallas_call(kernel, out_shape=jax.ShapeDtypeStruct((2, 128, 512), BF),...  86.3 us

profile of v5, /device:TPU:6, one launch (start us, length us, event | category | flops | bytes accessed | tf_op | source)
XLA Modules:
  0.0 87.7 jit_solution(11779591427143980185)
XLA Ops:
  0.6 86.3 %covariance.1 = bf16[2,128,512]{2,1,0:T(8,128)(2,1)S(1)} custom-call(bf16[16,128,512]{2,1,0:T(8,128)(2,1)} %ens_hbm.1, f32[128,512]{1,0:T(8,128)} %inc_hbm.1, f32[128,512]{1,0:T(8,128)} %obs_hbm.1, bf16[128,128]{1,0:T(8,128)(2,1)} %vert_hbm.1, bf16[12,128,128]{2,1,0:T(8,128)(2,1)} %table_hbm.1, s32[12,64]{1,0:T(8,128)} %bitcast.7), custom_call_target="tpu_custom_call" | custom-call | tf_op jit(solution)/shard_map/covariance/pallas_call | solution.py:312
  86.9 0.9 bitcast_convert_fusion
